TPU v7x, 32 devices: a whole 2x2x4 slice. The times are simulated.
32 devices in a mesh: fsdp: 2 (over x), ctx: 4 (over y, core), tp: 4 (over z).
Axes of the slice: x: 2, y: 2, z: 4, core: 2. Of those that a mesh axis runs over, the one named last changes fastest.
Arguments:
- tokens: bfloat16 [8, 512, 768], P(('fsdp', 'tp'), 'ctx'), may hold values from -6 to 6
- seg_ids: int32 [8, 512], P(('fsdp', 'tp')), may hold values from 0 to 2, never falling along the last dimension, each value on 1 to 384 neighbouring positions
- routes: int32 [8, 512, 2], P(('fsdp', 'tp'), 'ctx'), may hold values from 0 to 3, all different within a row; in each aligned block of 128 rows (0 to 127, 128 to 255, ..., all dimensions but the last counted through in order) at most 80 rows name the same one
- norm_attn: bfloat16 [768], P('fsdp'), may hold values from 0.5 to 1.5
- weight_qkv: bfloat16 [768, 2304], P('fsdp'), may hold values from -0.21875 to 0.21875
- weight_proj: bfloat16 [768, 768], P(None, 'fsdp'), may hold values from -0.875 to 0.875
- rel_table: float32 [12, 32], replicated, may hold values from -4 to 4
- norm_ffn: bfloat16 [768], P('fsdp'), may hold values from 0.5 to 1.5
- weight_router: bfloat16 [768, 4], P('fsdp'), may hold values from -0.21875 to 0.21875
- expert_up: bfloat16 [4, 768, 3072], P(None, 'fsdp', ('ctx', 'tp')), may hold values from -0.21875 to 0.21875
- expert_down: bfloat16 [4, 3072, 768], P(None, ('ctx', 'tp'), 'fsdp'), may hold values from -0.109375 to 0.109375
- cotangent: bfloat16 [8, 512, 768], P(('fsdp', 'tp'), 'ctx'), may hold values from -6 to 6
Outputs:
- output: bfloat16 [8, 512, 768], P(('fsdp', 'tp'), 'ctx')
- grad_tokens: float32 [8, 512, 768], P(('fsdp', 'tp'), 'ctx')
- grad_norm_attn: float32 [768], P('fsdp')
- grad_weight_qkv: float32 [768, 2304], P('fsdp')
- grad_weight_proj: float32 [768, 768], P(None, 'fsdp')
- grad_rel_table: float32 [12, 32], replicated
- grad_norm_ffn: float32 [768], P('fsdp')
- grad_weight_router: float32 [768, 4], P('fsdp')
- grad_expert_up: float32 [4, 768, 3072], P(None, 'fsdp', ('ctx', 'tp'))
- grad_expert_down: float32 [4, 3072, 768], P(None, ('ctx', 'tp'), 'fsdp')
Inputs may be any that keep to these rules, and one draw needn't show every extreme that they name: `seg_ids`: each group's 512 positions fall into at most 3 sequences whose numbers never fall along the positions; the longest has exactly 384 positions. `routes`: each token names two different experts. In each aligned block of 128 rows (the rows of one device) no expert is named more than 80 times, and in every draw some expert is named exactly 80 times in some block.
All inputs are finite; a program needn't handle non-finite values.
Results may differ from a plain program's by a relative error of at most 0.012.
Values may be sent and summed in bfloat16 or wider, within the bound.
A program may use at most 192 MiB of HBM per device.

v0:
```python
import jax
import jax.numpy as jnp
import numpy as np
from jax import lax
from jax.sharding import PartitionSpec as P

BUCKETS = 32
MAX_DISTANCE = 128
MOST = 80
EPSILON = 1e-06
MASK_FILL = -1e30


def bucket_bounds(buckets, far_reach):
    exact_count = buckets // 2
    bounds = []
    for number in range(1, buckets):
        if number <= exact_count:
            bounds.append(number)
        else:
            exponent = (number - exact_count) / (buckets - exact_count)
            bounds.append(int(np.ceil(exact_count * (far_reach / exact_count) ** exponent)))
    return np.array(bounds, dtype=np.int32)


def bucket_onehot(length):
    bounds = jnp.asarray(bucket_bounds(BUCKETS, MAX_DISTANCE))
    distance = jnp.arange(length, dtype=jnp.int32)
    which_bucket = jnp.sum((distance[:, None] >= bounds[None, :]).astype(jnp.int32), axis=1)
    return (which_bucket[:, None] == jnp.arange(BUCKETS, dtype=jnp.int32)[None, :]).astype(
        jnp.float32
    )


def spread_diagonals(vectors):
    heads_here, length = vectors.shape
    padded = jnp.concatenate([vectors[:, ::-1], jnp.zeros_like(vectors)], axis=1)
    repeated = jnp.tile(padded, (1, length))
    window = repeated[:, length - 1 : length - 1 + length * (2 * length - 1)]
    return window.reshape(heads_here, length, 2 * length - 1)[:, :, :length]


def slot_tables(route_ids, experts, capacity):
    flat_ids = route_ids.reshape(-1)
    assignments = flat_ids.shape[0]
    member = (flat_ids[:, None] == jnp.arange(experts, dtype=jnp.int32)[None, :]).astype(jnp.int32)
    before = jnp.cumsum(member, axis=0) - member
    slot_index = jnp.sum(before * member, axis=1)
    position = slot_index * experts + flat_ids
    filler = (
        jnp.full((capacity * experts,), assignments, jnp.int32)
        .at[position]
        .set(jnp.arange(assignments, dtype=jnp.int32))
    )
    return (position, filler)


def rms_scale(values):
    return lax.rsqrt(jnp.mean(values * values, axis=-1, keepdims=True) + EPSILON)


def local(
    tokens,
    seg_ids,
    routes,
    norm_attn,
    weight_qkv,
    weight_proj,
    rel_table,
    norm_ffn,
    weight_router,
    expert_up,
    expert_down,
    cotangent,
):
    row_count = tokens.shape[1]
    model_width = tokens.shape[2]
    head_count = rel_table.shape[0]
    head_size = model_width // head_count
    heads_here = head_count // lax.axis_size("ctx")
    expert_count = expert_up.shape[0]
    length = seg_ids.shape[1]
    score_scale = head_size ** (-0.5)
    ctx_index = lax.axis_index("ctx")
    head_width = heads_here * head_size
    gathered = (
        lax.all_gather(norm_attn, "fsdp", axis=0, tiled=True),
        lax.all_gather(weight_qkv, "fsdp", axis=0, tiled=True),
        lax.all_gather(weight_proj, "fsdp", axis=1, tiled=True),
        lax.all_gather(weight_router, "fsdp", axis=0, tiled=True),
        lax.all_gather(norm_ffn, "fsdp", axis=0, tiled=True),
        lax.all_gather(expert_up, "fsdp", axis=1, tiled=True),
        lax.all_gather(expert_down, "fsdp", axis=2, tiled=True),
    )
    gain_one, qkv_full, proj_full, router_full, gain_two, up_full, down_full = gathered
    inputs = tokens[0].astype(jnp.float32)
    scale_one = rms_scale(inputs)
    normed_one = (inputs * scale_one * gain_one.astype(jnp.float32)).astype(jnp.bfloat16)
    projected = jnp.dot(normed_one, qkv_full, preferred_element_type=jnp.float32).astype(
        jnp.bfloat16
    )
    by_head = lax.all_to_all(
        projected.reshape(row_count, 3, head_count, head_size),
        "ctx",
        split_axis=2,
        concat_axis=0,
        tiled=True,
    )
    query_rows = by_head[:, 0]
    key_rows = by_head[:, 1]
    value_rows = by_head[:, 2]
    table_here = lax.dynamic_slice_in_dim(rel_table, ctx_index * heads_here, heads_here, 0)
    onehot = bucket_onehot(length)
    bias_vector = jnp.dot(table_here, onehot.T, precision=lax.Precision.HIGHEST)
    bias_matrix = spread_diagonals(bias_vector)
    positions = jnp.arange(length, dtype=jnp.int32)
    segment = seg_ids[0]
    allowed = (segment[:, None] == segment[None, :]) & (positions[:, None] >= positions[None, :])
    block_count = length // length
    query_blocks = query_rows.reshape(block_count, length, heads_here, head_size)
    bias_blocks = jnp.moveaxis(bias_matrix.reshape(heads_here, block_count, length, length), 1, 0)
    mask_blocks = allowed.reshape(block_count, length, length)

    def block_scores(query_block, bias_block, mask_block):
        products = jnp.einsum(
            "qhd,khd->hqk", query_block, key_rows, preferred_element_type=jnp.float32
        )
        return jnp.where(mask_block[None], products * score_scale + bias_block, MASK_FILL)

    def forward_block(pieces):
        query_block, bias_block, mask_block = pieces
        scores = block_scores(query_block, bias_block, mask_block)
        row_peak = jnp.max(scores, axis=-1, keepdims=True)
        weights = jnp.exp(scores - row_peak)
        row_total = jnp.sum(weights, axis=-1, keepdims=True)
        low_probs = (weights / row_total).astype(jnp.bfloat16)
        attended = jnp.einsum(
            "hqk,khd->qhd", low_probs, value_rows, preferred_element_type=jnp.float32
        ).astype(jnp.bfloat16)
        return (attended, (row_peak + jnp.log(row_total))[..., 0])

    attended_blocks, log_totals = lax.map(forward_block, (query_blocks, bias_blocks, mask_blocks))
    attended_heads = attended_blocks.reshape(length, heads_here, head_size)
    back_tokens = lax.all_to_all(attended_heads, "ctx", split_axis=0, concat_axis=1, tiled=True)
    mixed_heads = back_tokens.reshape(row_count, model_width)
    attention = jnp.dot(mixed_heads, proj_full, preferred_element_type=jnp.float32)
    middle = inputs + attention
    scale_two = rms_scale(middle)
    normed_two = (middle * scale_two * gain_two.astype(jnp.float32)).astype(jnp.bfloat16)
    logits = jnp.dot(normed_two, router_full, preferred_element_type=jnp.float32)
    route_ids = routes[0]
    choose = (
        route_ids[:, :, None] == jnp.arange(expert_count, dtype=jnp.int32)[None, None, :]
    ).astype(jnp.float32)
    picked = jnp.sum(choose * logits[:, None, :], axis=2)
    gate_raw = jnp.exp(picked - jnp.max(picked, axis=1, keepdims=True))
    gate_weights = gate_raw / jnp.sum(gate_raw, axis=1, keepdims=True)
    position, filler = slot_tables(route_ids, expert_count, MOST)
    padded_rows = jnp.concatenate([normed_two, jnp.zeros((1, model_width), jnp.bfloat16)], axis=0)
    dispatched = padded_rows[filler // 2].reshape(MOST, expert_count, model_width)
    arrived = lax.all_gather(dispatched, ("ctx", "tp"), axis=0, tiled=True)
    pre_act = jnp.einsum("sed,edf->sef", arrived, up_full, preferred_element_type=jnp.float32)
    activated = jax.nn.gelu(pre_act).astype(jnp.bfloat16)
    row_block = activated
    expert_result = lax.psum_scatter(
        jnp.einsum("sef,efd->sed", row_block, down_full, preferred_element_type=jnp.float32),
        ("ctx", "tp"),
        scatter_dimension=0,
        tiled=True,
    )
    per_choice = expert_result.reshape(MOST * expert_count, model_width)[position].reshape(
        row_count, 2, model_width
    )
    result = middle + jnp.sum(gate_weights[:, :, None] * per_choice, axis=1)
    output = result.astype(jnp.bfloat16)[None]
    again = (
        lax.all_gather(norm_attn, "fsdp", axis=0, tiled=True),
        lax.all_gather(weight_qkv, "fsdp", axis=0, tiled=True),
        lax.all_gather(weight_proj, "fsdp", axis=1, tiled=True),
        lax.all_gather(weight_router, "fsdp", axis=0, tiled=True),
        lax.all_gather(norm_ffn, "fsdp", axis=0, tiled=True),
        lax.all_gather(expert_up, "fsdp", axis=1, tiled=True),
        lax.all_gather(expert_down, "fsdp", axis=2, tiled=True),
    )
    gain_first, qkv_again, proj_again, router_again, gain_second, up_again, down_again = again
    grad_out = cotangent[0].astype(jnp.float32)
    gate_dots = jnp.sum(grad_out[:, None, :] * per_choice, axis=2)
    grad_pick = gate_weights * (
        gate_dots - jnp.sum(gate_weights * gate_dots, axis=1, keepdims=True)
    )
    grad_logits = jnp.sum(grad_pick[:, :, None] * choose, axis=1)
    grad_choice = (
        (gate_weights[:, :, None] * grad_out[:, None, :])
        .astype(jnp.bfloat16)
        .reshape(2 * row_count, model_width)
    )
    padded_grads = jnp.concatenate([grad_choice, jnp.zeros((1, model_width), jnp.bfloat16)], axis=0)
    grad_slots = padded_grads[filler].reshape(MOST, expert_count, model_width)
    grad_arrived = lax.all_gather(grad_slots, ("ctx", "tp"), axis=0, tiled=True)
    grad_act = jnp.einsum(
        "sed,efd->sef", grad_arrived, down_again, preferred_element_type=jnp.float32
    )
    grad_down = jnp.einsum(
        "sef,sed->efd", activated, grad_arrived, preferred_element_type=jnp.float32
    )
    gelu_back = jax.vjp(jax.nn.gelu, pre_act)[1]
    grad_pre = gelu_back(grad_act)[0].astype(jnp.bfloat16)
    grad_up = jnp.einsum("sed,sef->edf", arrived, grad_pre, preferred_element_type=jnp.float32)
    row_block = grad_pre
    grad_dispatched = lax.psum_scatter(
        jnp.einsum("sef,edf->sed", row_block, up_again, preferred_element_type=jnp.float32),
        ("ctx", "tp"),
        scatter_dimension=0,
        tiled=True,
    )
    grad_normed_two = jnp.sum(
        grad_dispatched.reshape(MOST * expert_count, model_width)[position].reshape(
            row_count, 2, model_width
        ),
        axis=1,
    )
    router_float = router_again.astype(jnp.float32)
    grad_normed_two = grad_normed_two + jnp.dot(
        grad_logits, router_float.T, precision=lax.Precision.HIGHEST
    )
    grad_router = jnp.dot(
        normed_two.astype(jnp.float32).T, grad_logits, precision=lax.Precision.HIGHEST
    )
    weighted_two = grad_normed_two * gain_second.astype(jnp.float32)
    grad_gain_two = jnp.sum(grad_normed_two * middle * scale_two, axis=0)
    grad_middle = (
        grad_out
        + scale_two * weighted_two
        - middle * scale_two**3 * jnp.mean(weighted_two * middle, axis=1, keepdims=True)
    )
    grad_middle_low = grad_middle.astype(jnp.bfloat16)
    normed_group, grad_mid_group = (
        lax.all_gather(normed_one, "ctx", axis=0, tiled=True),
        lax.all_gather(grad_middle_low, "ctx", axis=0, tiled=True),
    )
    proj_rows = lax.dynamic_slice_in_dim(proj_again, ctx_index * head_width, head_width, 0)
    grad_attended = jnp.einsum(
        "te,de->td", grad_mid_group, proj_rows, preferred_element_type=jnp.float32
    ).astype(jnp.bfloat16)
    grad_proj_part = jnp.einsum(
        "td,te->de",
        attended_heads.reshape(length, head_width),
        grad_mid_group,
        preferred_element_type=jnp.float32,
    )
    grad_blocks = grad_attended.reshape(block_count, length, heads_here, head_size)

    def backward_block(running, pieces):
        key_sum, value_sum = running
        query_block, bias_block, mask_block, log_block, grad_block = pieces
        scores = block_scores(query_block, bias_block, mask_block)
        probs_float = jnp.exp(scores - log_block[..., None])
        low_probs = probs_float.astype(jnp.bfloat16)
        value_term = jnp.einsum(
            "hqk,qhd->khd", low_probs, grad_block, preferred_element_type=jnp.float32
        )
        grad_probs = jnp.einsum(
            "qhd,khd->hqk", grad_block, value_rows, preferred_element_type=jnp.float32
        )
        grad_scores = (
            probs_float * (grad_probs - jnp.sum(probs_float * grad_probs, axis=-1, keepdims=True))
        ).astype(jnp.bfloat16)
        query_term = (
            jnp.einsum("hqk,khd->qhd", grad_scores, key_rows, preferred_element_type=jnp.float32)
            * score_scale
        ).astype(jnp.bfloat16)
        key_term = (
            jnp.einsum("hqk,qhd->khd", grad_scores, query_block, preferred_element_type=jnp.float32)
            * score_scale
        )
        return ((key_sum + key_term, value_sum + value_term), (query_term, grad_scores))

    zero_rows = jnp.zeros((length, heads_here, head_size), jnp.float32)
    sums_kv, per_block = lax.scan(
        backward_block,
        (zero_rows, zero_rows),
        (query_blocks, bias_blocks, mask_blocks, log_totals, grad_blocks),
    )
    query_grads, score_grads = per_block
    grad_qkv_heads = jnp.stack(
        [
            query_grads.reshape(length, heads_here, head_size),
            sums_kv[0].astype(jnp.bfloat16),
            sums_kv[1].astype(jnp.bfloat16),
        ],
        axis=1,
    )
    grad_qkv_part = jnp.einsum(
        "td,tshk->dshk", normed_group, grad_qkv_heads, preferred_element_type=jnp.float32
    )
    grad_projected = lax.all_to_all(
        grad_qkv_heads, "ctx", split_axis=0, concat_axis=2, tiled=True
    ).reshape(row_count, 3 * model_width)
    score_matrix = (
        jnp.moveaxis(score_grads, 0, 1).reshape(heads_here, length, length).astype(jnp.float32)
    )
    spread_back = jax.vjp(spread_diagonals, bias_vector)[1]
    grad_vector = spread_back(score_matrix)[0]
    grad_table_here = jnp.dot(grad_vector, onehot, precision=lax.Precision.HIGHEST)
    table_term = lax.dynamic_update_slice_in_dim(
        jnp.zeros((head_count, BUCKETS), jnp.float32), grad_table_here, ctx_index * heads_here, 0
    )
    grad_normed_one = jnp.einsum(
        "te,de->td", grad_projected, qkv_again, preferred_element_type=jnp.float32
    )
    weighted_one = grad_normed_one * gain_first.astype(jnp.float32)
    grad_gain_one = jnp.sum(grad_normed_one * inputs * scale_one, axis=0)
    grad_tokens = (
        grad_middle
        + scale_one * weighted_one
        - inputs * scale_one**3 * jnp.mean(weighted_one * inputs, axis=1, keepdims=True)
    )
    shares = (
        lax.psum_scatter(grad_gain_one, "fsdp", scatter_dimension=0, tiled=True),
        lax.psum_scatter(grad_qkv_part, "fsdp", scatter_dimension=0, tiled=True),
        lax.psum_scatter(grad_proj_part, "fsdp", scatter_dimension=1, tiled=True),
        lax.psum_scatter(grad_router, "fsdp", scatter_dimension=0, tiled=True),
        lax.psum_scatter(grad_gain_two, "fsdp", scatter_dimension=0, tiled=True),
        lax.psum_scatter(grad_up, "fsdp", scatter_dimension=1, tiled=True),
        lax.psum_scatter(grad_down, "fsdp", scatter_dimension=2, tiled=True),
    )
    qkv_share = shares[1]
    own_rows = qkv_share.shape[0]
    qkv_placed = lax.dynamic_update_slice_in_dim(
        jnp.zeros((own_rows, 3, head_count, head_size), jnp.float32),
        qkv_share,
        ctx_index * heads_here,
        2,
    ).reshape(own_rows, 3 * model_width)
    proj_share = shares[2]
    proj_placed = lax.dynamic_update_slice_in_dim(
        jnp.zeros((model_width, proj_share.shape[1]), jnp.float32),
        proj_share,
        ctx_index * head_width,
        0,
    )
    summed = lax.psum((shares[0], qkv_placed, proj_placed, shares[3], shares[4]), ("ctx", "tp"))
    table_grad = lax.psum(table_term, ("fsdp", "ctx", "tp"))
    return (
        output,
        grad_tokens[None],
        summed[0],
        summed[1],
        summed[2],
        table_grad,
        summed[4],
        summed[3],
        shares[5],
        shares[6],
    )


def solution(mesh):
    in_specs = (
        P(("fsdp", "tp"), "ctx", None),
        P(("fsdp", "tp"), None),
        P(("fsdp", "tp"), "ctx", None),
        P("fsdp"),
        P("fsdp", None),
        P(None, "fsdp"),
        P(),
        P("fsdp"),
        P("fsdp", None),
        P(None, "fsdp", ("ctx", "tp")),
        P(None, ("ctx", "tp"), "fsdp"),
        P(("fsdp", "tp"), "ctx", None),
    )
    out_specs = (
        P(("fsdp", "tp"), "ctx", None),
        P(("fsdp", "tp"), "ctx", None),
        P("fsdp"),
        P("fsdp", None),
        P(None, "fsdp"),
        P(),
        P("fsdp"),
        P("fsdp", None),
        P(None, "fsdp", ("ctx", "tp")),
        P(None, ("ctx", "tp"), "fsdp"),
    )
    return jax.shard_map(local, mesh=mesh, in_specs=in_specs, out_specs=out_specs, check_vma=False)
```

profile of v0, /device:TPU:0, one launch (start us, length us, event | category | flops | bytes accessed | tf_op | source)
XLA Modules:
  0.0 897.2 jit_solution(6429418993881922095)
XLA Ops:
  11.4 5.2 all-gather
  16.7 4.4 all-gather.1
  24.1 3.4 broadcast_bitcast_fusion
  27.6 7.1 copy.178
  34.7 6.6 slice.39
  41.3 13.2 %reshape.303 = f32[3,512,1023]{2,1,0:T(8,128)} reshape(f32[3,523776]{1,0:T(4,128)} %slice.39) | data formatting | bytes 12570624 | tf_op jit(solution)/shard_map/reshape | solution.py:40
  61.8 2.7 convolution_convert_fusion
  65.6 3.6 all-to-all-start
  70.7 8.0 all-to-all-done
  80.2 3.0 fusion.61
  88.4 4.0 all-to-all-start.1
  94.5 3.3 all-to-all-done.1
  117.3 4.5 all_gather.44
  132.9 4.2 gather_fusion.2
  140.9 44.0 %all-gather.13.cloned.1.call-done = bf16[1280,4,768]{2,0,1:T(8,128)(2,1)} async-done(((bf16[80,4,768]{2,0,1:T(8,128)(2,1)}), bf16[1280,4,768]{2,0,1:T(8,128)(2,1)}) %all-gather.13.cloned.1.call-update) | async-done | bytes 7864336 | tf_op jit(solution)/shard_map/all_gather | solution.py:161
  184.9 8.1 fusion.63
  193.0 14.4 %all-gather.17.cloned.1.call-done = bf16[4,192,768]{2,1,0:T(8,128)(2,1)} async-done(((bf16[4,192,384]{2,1,0:T(8,128)(2,1)}), bf16[4,192,768]{2,1,0:T(8,128)(2,1)}) %all-gather.17.cloned.1.call-update) | async-done | bytes 1179664 | tf_op jit(solution)/shard_map/all_gather | solution.py:93
  207.5 10.3 %convolution_bitcast_fusion.1 = f32[1280,4,768]{2,0,1:T(8,128)} fusion(bf16[4,192,768]{2,1,0:T(8,128)(2,1)} %all-gather.17.cloned.1.call-done, f32[4,1280,192]{1,2,0:T(8,128)} %fusion.63), kind=kOutput, calls=%fused_computation.6 | convolution fusion | flops 1518796800 | bytes 20840448 | tf_op jit(solution)/shard_map/sef,efd->sed/dot_general | solution.py:166
  218.0 63.8 %all-gather.19.cloned.1.call-done = bf16[1280,4,768]{2,0,1:T(8,128)(2,1)} async-done(((bf16[80,4,768]{2,0,1:T(8,128)(2,1)}), bf16[1280,4,768]{2,0,1:T(8,128)(2,1)}) %all-gather.19.cloned.1.call-update) | async-done | bytes 7864336 | tf_op jit(solution)/shard_map/all_gather | solution.py:199
  281.9 8.6 fusion.6
  291.7 10.6 %convolution_bitcast_fusion = f32[1280,4,768]{2,0,1:T(8,128)} fusion(bf16[1280,4,192]{0,2,1:T(8,128)(2,1)S(1)} %fusion.6, bf16[4,768,192]{1,2,0:T(8,128)(2,1)S(1)} %copy-done.7), kind=kOutput, calls=%fused_computation.5 | convolution fusion | flops 1509949440 | bytes 18874368 | tf_op jit(solution)/shard_map/sef,edf->sed/dot_general | solution.py:211
  303.6 9.7 %all_gather.50 = bf16[512,768]{1,0:T(8,128)(2,1)} all-gather(bf16[128,768]{1,0:T(8,128)(2,1)} %copy-done.19), channel_id=1, replica_groups=mesh['fsdp'=2,'ctx'=4,'tp'=4] {'ctx'}, dimensions={0}, use_global_device_ids=true | all-gather | bytes 983040 | tf_op jit(solution)/shard_map/all_gather | solution.py:238
  314.0 127.2 %reduce-scatter.10.cloned.1.call-done = f32[80,4,768]{2,0,1:T(8,128)} async-done(((f32[1280,4,768]{2,0,1:T(8,128)}), f32[80,4,768]{2,0,1:T(8,128)}) %reduce-scatter.10.cloned.1.call-update) | async-done | bytes 983056 | tf_op jit(solution)/shard_map/reduce_scatter | solution.py:165
  441.2 2.8 copy.151
  446.4 3.6 gather_fusion.1
  452.6 3.5 multiply_reduce_fusion.1
  459.1 142.7 %reduce-scatter.12.cloned.1.call-done = f32[80,4,768]{2,0,1:T(8,128)} async-done(((f32[1280,4,768]{2,0,1:T(8,128)}), f32[80,4,768]{2,0,1:T(8,128)}) %reduce-scatter.12.cloned.1.call-update) | async-done | bytes 983056 | tf_op jit(solution)/shard_map/reduce_scatter | solution.py:210
  601.8 2.8 copy.154
  607.1 3.7 gather_fusion.3
  613.2 2.8 reduce_sum.172
  620.4 8.6 all_gather.49
  641.4 3.9 reduce-scatter.16.cloned.1.call-done
  648.1 28.3 %reduce-scatter.14.cloned.1.call-done = f32[384,3,3,64]{0,3,2,1:T(8,128)} async-done(((f32[768,3,3,64]{0,3,2,1:T(8,128)}), f32[384,3,3,64]{0,3,2,1:T(8,128)}) %reduce-scatter.14.cloned.1.call-update) | async-done | bytes 884752 | tf_op jit(solution)/shard_map/reduce_scatter | solution.py:320
  679.5 7.0 fusion.67
  688.0 7.8 fusion.57
  703.2 7.6 reshape.380
  710.9 5.7 reshape.314
  718.7 4.4 all-to-all-start.2
  723.1 4.6 pad_convert_fusion
  727.7 3.3 bitcast_reduce_fusion
  734.8 39.7 %psum.45 = f32[12,32]{1,0:T(8,128)} all-reduce(f32[12,32]{1,0:T(8,128)S(1)} %dynamic_update_slice.22), channel_id=1, replica_groups=mesh['fsdp'=2,'ctx'=4,'tp'=4] {'fsdp','ctx','tp'}, use_global_device_ids=true, to_apply=%region_30.31 | all-reduce | flops 384 | bytes 3072 | tf_op jit(solution)/shard_map/psum | solution.py:343
  775.5 3.9 reshape.385
  779.4 3.4 copy.162
  782.8 3.9 fusion.37
  786.7 5.3 all-reduce.9
  792.1 60.5 %all-reduce.7 = (f32[384]{0:T(512)}, f32[384]{0:T(512)}, f32[384,4]{0,1:T(4,128)}) all-reduce(f32[384]{0:T(512)S(1)} %dynamic-slice.3, f32[384]{0:T(512)S(1)} %dynamic-slice.5, f32[384,4]{0,1:T(4,128)S(1)} %copy.175), channel_id=1, replica_groups=mesh['fsdp'=2,'ctx'=4,'tp'=4] {'ctx','tp'}, use_global_device_ids=true, to_apply=%region_24.25 | all-reduce | flops 2304 | bytes 18432 | tf_op jit(solution)/shard_map/psum | solution.py:342
  855.4 5.2 copy.164
  860.6 28.8 %reduce-scatter.20.cloned.1.call-done = f32[4,192,384]{2,1,0:T(8,128)} async-done(((f32[4,192,768]{2,1,0:T(8,128)}), f32[4,192,384]{2,1,0:T(8,128)}) %reduce-scatter.20.cloned.1.call-update) | async-done | bytes 1179664 | tf_op jit(solution)/shard_map/reduce_scatter | solution.py:325
  (235 shorter events, 118.3 us)
Async XLA Ops:
  7.2 14.6 %copy-start = (f32[12,32]{1,0:T(8,128)S(1)}, f32[12,32]{1,0:T(8,128)}, u32[]{:S(2)}) copy-start(f32[12,32]{1,0:T(8,128)} %param.19) | copy-start | bytes 4612
  7.2 13.9 %copy-start.43 = (s32[31]{0:T(128)S(1)}, s32[31]{0:T(128)}, u32[]{:S(2)}) copy-start(s32[31]{0:T(128)} %constant.127.clone) | copy-start | bytes 376
  7.2 3.5 copy-start.14
  7.2 4.2 copy-start.41
  7.2 9.4 %copy-start.42 = (bf16[384]{0:T(512)(128)(2,1)S(1)}, bf16[384]{0:T(512)(128)(2,1)}, u32[]{:S(2)}) copy-start(bf16[384]{0:T(512)(128)(2,1)} %param.20) | copy-start | bytes 2308
  7.2 54.5 %all-gather.9.cloned.1.call-start = ((), (), s32[]{:S(2)}) async-start(), calls=%async_computation.10 | async-start | bytes 5308416 | tf_op jit(solution)/shard_map/all_gather | solution.py:88
  8.0 93.8 %all-gather.11.cloned.1.call-start = ((), (), s32[]{:S(2)}) async-start(), calls=%async_computation.11 | async-start | bytes 1769472 | tf_op jit(solution)/shard_map/all_gather | solution.py:89
  8.7 132.2 %all-gather.15.cloned.1.call-start = ((), (), s32[]{:S(2)}) async-start(), calls=%async_computation.13 | async-start | bytes 1769472 | tf_op jit(solution)/shard_map/all_gather | solution.py:92
  11.4 47.3 %copy-start.36 = (f32[128]{0:T(128)}, f32[128]{0:T(128)S(1)}, u32[]{:S(2)}) copy-start(f32[128]{0:T(128)S(1)} %get-tuple-element.139) | copy-start | bytes 1540
  16.7 42.1 %copy-start.26 = (f32[768]{0:T(1024)}, f32[768]{0:T(1024)S(1)}, u32[]{:S(2)}) copy-start(f32[768]{0:T(1024)S(1)} %reshape.367) | copy-start | bytes 9220
  54.5 1.9 slice-start
  58.9 2.9 copy-start.19
  60.7 9.1 %copy-start.33 = (s32[1,512]{1,0:T(1,128)S(1)}, s32[1,512]{1,0:T(1,128)}, u32[]{:S(2)}) copy-start(s32[1,512]{1,0:T(1,128)} %param.14) | copy-start | bytes 6148
  65.6 13.2 %all-to-all-start = ((bf16[128,3,12,64]{0,3,1,2:T(8,128)(2,1)}), bf16[128,3,12,64]{0,3,1,2:T(8,128)(2,1)S(1)}, u32[]{:S(2)}, u32[]{:S(2)}) async-start(bf16[128,3,12,64]{0,3,1,2:T(8,128)(2,1)} %copy.136), calls=%async_computation | async-start | bytes 1179648 | tf_op jit(solution)/shard_map/all_to_all | solution.py:102
  85.3 18.9 %copy-start.22 = (bf16[3,64,512]{2,1,0:T(8,128)(2,1)}, bf16[3,64,512]{2,1,0:T(8,128)(2,1)S(1)}, u32[]{:S(2)}) copy-start(bf16[3,64,512]{2,1,0:T(8,128)(2,1)S(1)} %fusion.19) | copy-start | bytes 589828
  88.4 9.4 %all-to-all-start.1 = ((bf16[4,2,12288]{2,1,0:T(2,128)(2,1)}), bf16[4,2,12288]{2,1,0:T(2,128)(2,1)}, u32[]{:S(2)}, u32[]{:S(2)}) async-start(bf16[4,2,12288]{2,1,0:T(2,128)(2,1)} %reshape.382), calls=%async_computation.1 | async-start | bytes 393216 | tf_op jit(solution)/shard_map/all_to_all | solution.py:144
  92.4 92.5 %all-gather.13.cloned.1.call-start = ((), (), s32[]{:S(2)}) async-start(), calls=%async_computation.12 | async-start | bytes 8355840 | tf_op jit(solution)/shard_map/all_gather | solution.py:161
  93.2 15.0 %copy-start.24 = (f32[768]{0:T(1024)}, f32[768]{0:T(1024)S(1)}, u32[]{:S(2)}) copy-start(f32[768]{0:T(1024)S(1)} %reshape.368) | copy-start | bytes 9220
  112.0 95.5 %all-gather.17.cloned.1.call-start = ((), (), s32[]{:S(2)}) async-start(), calls=%async_computation.14 | async-start | bytes 1769472 | tf_op jit(solution)/shard_map/all_gather | solution.py:93
  112.6 169.3 %all-gather.19.cloned.1.call-start = ((), (), s32[]{:S(2)}) async-start(), calls=%async_computation.16 | async-start | bytes 8355840 | tf_op jit(solution)/shard_map/all_gather | solution.py:199
  121.7 15.3 %copy-start.28 = (bf16[768,4]{0,1:T(4,128)(2,1)}, bf16[768,4]{0,1:T(4,128)(2,1)S(1)}, u32[]{:S(2)}) copy-start(bf16[768,4]{0,1:T(4,128)(2,1)S(1)} %all_gather.44) | copy-start | bytes 18436
  140.9 300.3 %reduce-scatter.10.cloned.1.call-start = ((), (), s32[]{:S(2)}) async-start(), calls=%async_computation.15 | async-start | bytes 16711680 | tf_op jit(solution)/shard_map/reduce_scatter | solution.py:165
  217.8 384.0 %reduce-scatter.12.cloned.1.call-start = ((), (), s32[]{:S(2)}) async-start(), calls=%async_computation.17 | async-start | bytes 16711680 | tf_op jit(solution)/shard_map/reduce_scatter | solution.py:210
  281.9 9.8 %copy-start.7 = (bf16[4,768,192]{1,2,0:T(8,128)(2,1)S(1)}, bf16[4,768,192]{1,2,0:T(8,128)(2,1)}, u32[]{:S(2)}) copy-start(bf16[4,768,192]{1,2,0:T(8,128)(2,1)} %all-gather.15.cloned.1.call-done) | copy-start | bytes 3538948
  302.3 343.0 %reduce-scatter.16.cloned.1.call-start = ((), (), s32[]{:S(2)}) async-start(), calls=%async_computation.19 | async-start | bytes 884736 | tf_op jit(solution)/shard_map/reduce_scatter | solution.py:321
  450.0 7.0 copy-start.29
  450.0 7.0 copy-start.32
  607.1 8.9 copy-start.11
  607.1 8.9 copy-start.25
  616.0 13.8 %copy-start.23 = (bf16[3,64,512]{2,1,0:T(8,128)(2,1)S(1)}, bf16[3,64,512]{2,1,0:T(8,128)(2,1)}, u32[]{:S(2)}) copy-start(bf16[3,64,512]{2,1,0:T(8,128)(2,1)} %copy-done.22) | copy-start | bytes 589828
  631.0 45.4 %reduce-scatter.14.cloned.1.call-start = ((), (), s32[]{:S(2)}) async-start(), calls=%async_computation.18 | async-start | bytes 2654208 | tf_op jit(solution)/shard_map/reduce_scatter | solution.py:320
  636.4 1.9 copy-start.18
  637.4 2.8 copy-start.17
  640.2 134.3 %reduce-scatter.22.cloned.1.call-start = ((), (), s32[]{:S(2)}) async-start(), calls=%async_computation.22 | async-start | bytes 589824
  641.4 214.0 %all-reduce.12.cloned.1.call-start = ((), (), s32[]{:S(2)}) async-start(), calls=%async_computation.23 | async-start | bytes 9437184 | tf_op jit(solution)/shard_map/psum | solution.py:342
  677.6 1.8 copy-start.5
  679.4 7.3 copy-start.44
  679.5 181.2 %reduce-scatter.18.cloned.1.call-start = ((), (), s32[]{:S(2)}) async-start(), calls=%async_computation.20 | async-start | bytes 3538944 | tf_op jit(solution)/shard_map/reduce_scatter | solution.py:324
  686.5 202.9 %reduce-scatter.20.cloned.1.call-start = ((), (), s32[]{:S(2)}) async-start(), calls=%async_computation.21 | async-start | bytes 3538944 | tf_op jit(solution)/shard_map/reduce_scatter | solution.py:325
  695.8 3.0 copy-start.13
  710.9 5.7 copy-start.9
  718.7 56.8 %all-to-all-start.2 = ((bf16[4,2,36864]{2,1,0:T(2,128)(2,1)}), bf16[4,2,36864]{2,1,0:T(2,128)(2,1)}, u32[]{:S(2)}, u32[]{:S(2)}) async-start(bf16[4,2,36864]{2,1,0:T(2,128)(2,1)} %reshape.384), calls=%async_computation.4 | async-start | bytes 1179648 | tf_op jit(solution)/shard_map/all_to_all | solution.py:296
  727.7 4.7 copy-start.40
  731.0 51.8 %copy-start.4 = (bf16[768,2304]{1,0:T(8,128)(2,1)S(1)}, bf16[768,2304]{1,0:T(8,128)(2,1)}, u32[]{:S(2)}) copy-start(bf16[768,2304]{1,0:T(8,128)(2,1)} %all-gather.9.cloned.1.call-done) | copy-start | bytes 10616836
  731.0 51.8 %copy-start.27 = (f32[768]{0:T(1024)S(1)}, f32[768]{0:T(1024)}, u32[]{:S(2)}) copy-start(f32[768]{0:T(1024)} %copy-done.26) | copy-start | bytes 9220
  779.4 7.3 copy-start.31
  855.4 35.1 %copy-start.1 = (f32[12,32]{1,0:T(8,128)S(1)}, f32[12,32]{1,0:T(8,128)}, u32[]{:S(2)}) copy-start(f32[12,32]{1,0:T(8,128)} %param.19) | copy-start | bytes 4612
  855.4 34.1 %copy-start.20 = (f32[768,384]{1,0:T(8,128)S(1)}, f32[768,384]{1,0:T(8,128)}, u32[]{:S(2)}) copy-start(f32[768,384]{1,0:T(8,128)} %get-tuple-element.156) | copy-start | bytes 3538948
  (15 other events, 14.2 us)
Sparse Core Ops, SparseCore 0:
  9.6 52.0 all-gather.8
  63.3 22.7 all-gather.10
  87.7 22.7 all-gather.14
  113.3 71.5 all-gather.12
  186.3 21.1 all-gather.16
  210.2 71.5 all-gather.18
  286.0 155.1 reduce-scatter.9
  445.8 155.9 reduce-scatter.11
  631.1 14.1 reduce-scatter.15
  648.1 28.2 reduce-scatter.13
  678.6 13.0 reduce-scatter.21
  696.3 118.0 all-reduce.11
  817.3 34.6 reduce-scatter.17
  854.7 34.7 reduce-scatter.19
where the time goes:
time: 905 us; the launch traced here: 897 us
  waiting for transfers between devices  468 us (52%)
  local copies, waits for them, and re-layouts  146 us (16%)
  blocking collectives  138 us (15%)
  matrix products  79.4 us (9%)
  other arithmetic  37 us (4%)
  between operations  15.4 us (2%)
  starting transfers between devices  13.4 us (1%)
    reduce_scatter x1, waiting for transfers between devices, local(): lax.psum_scatter(jnp.einsum('sef,edf->sed', row_block, up_again, preferre...  143 us
    reduce_scatter x1, waiting for transfers between devices, local(): lax.psum_scatter(jnp.einsum('sef,efd->sed', row_block, down_full, preferr...  127 us
    all_gather x1, waiting for transfers between devices, local(): grad_arrived = lax.all_gather(grad_slots, ('ctx', 'tp'), axis=0, tiled=True)  63.8 us
    psum x1, blocking collectives, local(): lax.psum((shares[0], qkv_placed, proj_placed, shares[3], shares[4]), ('ct...  60.5 us
    unnamed x108, local copies, waits for them, and re-layouts  51.7 us
    all_gather x1, waiting for transfers between devices, local(): arrived = lax.all_gather(dispatched, ('ctx', 'tp'), axis=0, tiled=True)  44 us
    psum x1, blocking collectives, local(): table_grad = lax.psum(table_term, ('fsdp', 'ctx', 'tp'))  39.7 us
    reduce_scatter x1, waiting for transfers between devices, local(): lax.psum_scatter(grad_down, 'fsdp', scatter_dimension=2, tiled=True)  28.8 us
  transfers between devices with their start and end apart: 17, of which 11 were waited for; matrix products, arithmetic and copies ran while one was open for 25% of the time, Pallas kernels for 0%

commit v1 on v0

--- a/solution.py
+++ b/solution.py
@@ -339,7 +339,9 @@
         ctx_index * head_width,
         0,
     )
-    summed = lax.psum((shares[0], qkv_placed, proj_placed, shares[3], shares[4]), ("ctx", "tp"))
+    summed = lax.psum(
+        lax.psum((shares[0], qkv_placed, proj_placed, shares[3], shares[4]), "tp"), "ctx"
+    )
     table_grad = lax.psum(table_term, ("fsdp", "ctx", "tp"))
     return (
         output,

time: 905 us -> 1060 us (1.17)
  waiting for transfers between devices: 468 us -> 656 us
  blocking collectives: 138 us -> 107 us
    psum x1 -> x2, waiting for transfers between devices: 0.01 us -> 171 us  [the longest x1 171 us: local(): lax.psum((shares[0], qkv_placed, proj_placed, shares[3], shares[4]), 'tp')]
    psum x1 -> x2, blocking collectives: 60.5 us -> 29 us  [the longest x1 17.5 us: local(): lax.psum((shares[0], qkv_placed, proj_placed, shares[3], shares[4]), 'tp')]
  transfers between devices with their start and end apart: 17 -> 18, of which waited for: 11 -> 13; matrix products, arithmetic and copies ran while one was open for 25% -> 22% of each run, Pallas kernels for 0% -> 0%
where the time goes in v1:
time: 1060 us; the launch traced here: 1050 us
  waiting for transfers between devices  656 us (62%)
  local copies, waits for them, and re-layouts  146 us (14%)
  blocking collectives  107 us (10%)
  matrix products  79.8 us (8%)
  other arithmetic  37 us (3%)
  between operations  15.4 us (1%)
  starting transfers between devices  13.4 us (1%)
    psum x1, waiting for transfers between devices, local(): lax.psum((shares[0], qkv_placed, proj_placed, shares[3], shares[4]), 'tp')  171 us
    reduce_scatter x1, waiting for transfers between devices, local(): lax.psum_scatter(jnp.einsum('sef,edf->sed', row_block, up_again, preferre...  143 us
    reduce_scatter x1, waiting for transfers between devices, local(): lax.psum_scatter(jnp.einsum('sef,efd->sed', row_block, down_full, preferr...  127 us
    all_gather x1, waiting for transfers between devices, local(): grad_arrived = lax.all_gather(grad_slots, ('ctx', 'tp'), axis=0, tiled=True)  63.8 us
    unnamed x108, local copies, waits for them, and re-layouts  51.6 us
    all_gather x1, waiting for transfers between devices, local(): arrived = lax.all_gather(dispatched, ('ctx', 'tp'), axis=0, tiled=True)  44 us
    psum x1, blocking collectives, local(): table_grad = lax.psum(table_term, ('fsdp', 'ctx', 'tp'))  40.4 us
    reduce_scatter x1, waiting for transfers between devices, local(): lax.psum_scatter(grad_down, 'fsdp', scatter_dimension=2, tiled=True)  37.4 us
  transfers between devices with their start and end apart: 18, of which 13 were waited for; matrix products, arithmetic and copies ran while one was open for 22% of the time, Pallas kernels for 0%

profile of v1, /device:TPU:0, one launch (start us, length us, event | category | flops | bytes accessed | tf_op | source)
XLA Modules:
  0.0 1054.0 jit_solution(8961723569902882844)
XLA Ops:
  11.4 5.2 all-gather
  16.7 4.4 all-gather.1
  24.1 3.4 broadcast_bitcast_fusion
  27.6 7.1 copy.178
  34.7 6.6 slice.39
  41.3 13.2 %reshape.303 = f32[3,512,1023]{2,1,0:T(8,128)} reshape(f32[3,523776]{1,0:T(4,128)} %slice.39) | data formatting | bytes 12570624 | tf_op jit(solution)/shard_map/reshape | solution.py:40
  65.6 3.6 all-to-all-start
  70.7 8.0 all-to-all-done
  80.2 3.0 fusion.61
  88.4 4.0 all-to-all-start.1
  94.5 3.3 all-to-all-done.1
  117.3 4.5 all_gather.44
  132.9 4.2 gather_fusion.2
  141.0 44.0 %all-gather.13.cloned.1.call-done = bf16[1280,4,768]{2,0,1:T(8,128)(2,1)} async-done(((bf16[80,4,768]{2,0,1:T(8,128)(2,1)}), bf16[1280,4,768]{2,0,1:T(8,128)(2,1)}) %all-gather.13.cloned.1.call-update) | async-done | bytes 7864336 | tf_op jit(solution)/shard_map/all_gather | solution.py:161
  184.9 8.1 fusion.63
  193.0 14.4 %all-gather.17.cloned.1.call-done = bf16[4,192,768]{2,1,0:T(8,128)(2,1)} async-done(((bf16[4,192,384]{2,1,0:T(8,128)(2,1)}), bf16[4,192,768]{2,1,0:T(8,128)(2,1)}) %all-gather.17.cloned.1.call-update) | async-done | bytes 1179664 | tf_op jit(solution)/shard_map/all_gather | solution.py:93
  207.5 10.3 convolution_bitcast_fusion.1
  218.0 63.8 %all-gather.19.cloned.1.call-done = bf16[1280,4,768]{2,0,1:T(8,128)(2,1)} async-done(((bf16[80,4,768]{2,0,1:T(8,128)(2,1)}), bf16[1280,4,768]{2,0,1:T(8,128)(2,1)}) %all-gather.19.cloned.1.call-update) | async-done | bytes 7864336 | tf_op jit(solution)/shard_map/all_gather | solution.py:199
  281.9 8.6 fusion.6
  291.7 10.6 %convolution_bitcast_fusion = f32[1280,4,768]{2,0,1:T(8,128)} fusion(bf16[1280,4,192]{0,2,1:T(8,128)(2,1)S(1)} %fusion.6, bf16[4,768,192]{1,2,0:T(8,128)(2,1)S(1)} %copy-done.8), kind=kOutput, calls=%fused_computation.5 | convolution fusion | flops 1509949440 | bytes 18874368 | tf_op jit(solution)/shard_map/sef,edf->sed/dot_general | solution.py:211
  303.6 9.7 all_gather.50
  314.0 127.2 %reduce-scatter.10.cloned.1.call-done = f32[80,4,768]{2,0,1:T(8,128)} async-done(((f32[1280,4,768]{2,0,1:T(8,128)}), f32[80,4,768]{2,0,1:T(8,128)}) %reduce-scatter.10.cloned.1.call-update) | async-done | bytes 983056 | tf_op jit(solution)/shard_map/reduce_scatter | solution.py:165
  446.4 3.6 gather_fusion.1
  452.6 3.5 multiply_reduce_fusion.1
  459.1 142.7 %reduce-scatter.12.cloned.1.call-done = f32[80,4,768]{2,0,1:T(8,128)} async-done(((f32[1280,4,768]{2,0,1:T(8,128)}), f32[80,4,768]{2,0,1:T(8,128)}) %reduce-scatter.12.cloned.1.call-update) | async-done | bytes 983056 | tf_op jit(solution)/shard_map/reduce_scatter | solution.py:210
  607.1 3.7 gather_fusion.3
  613.2 2.8 reduce_sum.172
  620.4 8.6 all_gather.49
  640.2 5.1 reduce-scatter.16.cloned.1.call-done
  648.1 28.3 %reduce-scatter.14.cloned.1.call-done = f32[384,3,3,64]{0,3,2,1:T(8,128)} async-done(((f32[768,3,3,64]{0,3,2,1:T(8,128)}), f32[384,3,3,64]{0,3,2,1:T(8,128)}) %reduce-scatter.14.cloned.1.call-update) | async-done | bytes 884752 | tf_op jit(solution)/shard_map/reduce_scatter | solution.py:320
  681.8 170.5 %all-reduce.15.cloned.1.call-done = (f32[384,2304]{0,1:T(8,128)}, f32[768,384]{1,0:T(8,128)}) async-done(((f32[384,2304]{0,1:T(8,128)}, f32[768,384]{1,0:T(8,128)}), (f32[384,2304]{0,1:T(8,128)}, f32[768,384]{1,0:T(8,128)})) %all-reduce.15.cloned.1.call-update) | async-done | bytes 4718608 | tf_op jit(solution)/shard_map/psum | solution.py:343
  852.4 6.5 fusion.67
  860.3 7.7 fusion.57
  875.3 7.5 reshape.380
  882.9 5.7 reshape.314
  890.7 4.4 all-to-all-start.2
  895.1 4.6 pad_convert_fusion
  899.7 3.3 bitcast_reduce_fusion
  906.8 40.4 %psum.83 = f32[12,32]{1,0:T(8,128)} all-reduce(f32[12,32]{1,0:T(8,128)S(1)} %dynamic_update_slice.22), channel_id=1, replica_groups=mesh['fsdp'=2,'ctx'=4,'tp'=4] {'fsdp','ctx','tp'}, use_global_device_ids=true, to_apply=%region_33.34 | all-reduce | flops 384 | bytes 3072 | tf_op jit(solution)/shard_map/psum | solution.py:345
  948.2 3.9 reshape.385
  952.1 3.3 copy.162
  955.3 3.9 fusion.37
  959.2 5.3 all-reduce.11
  964.7 17.5 %all-reduce.7 = (f32[384]{0:T(512)S(1)}, f32[384]{0:T(512)S(1)}, f32[384,4]{0,1:T(4,128)S(1)}) all-reduce(f32[384]{0:T(512)S(1)} %dynamic-slice.3, f32[384]{0:T(512)S(1)} %dynamic-slice.5, f32[384,4]{0,1:T(4,128)S(1)} %copy.175), channel_id=1, replica_groups=mesh['fsdp'=2,'ctx'=4,'tp'=4] {'tp'}, use_global_device_ids=true, to_apply=%region_24.25 | all-reduce | flops 2304 | bytes 18432 | tf_op jit(solution)/shard_map/psum | solution.py:343
  982.2 11.5 %all-reduce.9 = (f32[384]{0:T(512)}, f32[384]{0:T(512)}, f32[384,4]{0,1:T(4,128)}) all-reduce(f32[384]{0:T(512)S(1)} %get-tuple-element.126, f32[384]{0:T(512)S(1)} %get-tuple-element.127, f32[384,4]{0,1:T(4,128)S(1)} %get-tuple-element.128), channel_id=1, replica_groups=mesh['fsdp'=2,'ctx'=4,'tp'=4] {'ctx'}, use_global_device_ids=true, to_apply=%region_25.26 | all-reduce | flops 2304 | bytes 18432 | tf_op jit(solution)/shard_map/psum | solution.py:342
  996.4 5.2 copy.164
  1001.6 7.2 reduce-scatter.18.cloned.1.call-done
  1008.8 37.4 %reduce-scatter.20.cloned.1.call-done = f32[4,192,384]{2,1,0:T(8,128)} async-done(((f32[4,192,768]{2,1,0:T(8,128)}), f32[4,192,384]{2,1,0:T(8,128)}) %reduce-scatter.20.cloned.1.call-update) | async-done | bytes 1179664 | tf_op jit(solution)/shard_map/reduce_scatter | solution.py:325
  (239 shorter events, 127.4 us)
Async XLA Ops:
  7.2 14.6 %copy-start = (f32[12,32]{1,0:T(8,128)S(1)}, f32[12,32]{1,0:T(8,128)}, u32[]{:S(2)}) copy-start(f32[12,32]{1,0:T(8,128)} %param.19) | copy-start | bytes 4612
  7.2 13.9 %copy-start.43 = (s32[31]{0:T(128)S(1)}, s32[31]{0:T(128)}, u32[]{:S(2)}) copy-start(s32[31]{0:T(128)} %constant.127.clone) | copy-start | bytes 376
  7.2 3.5 copy-start.15
  7.2 4.2 copy-start.41
  7.2 9.4 copy-start.42
  7.2 54.5 %all-gather.9.cloned.1.call-start = ((), (), s32[]{:S(2)}) async-start(), calls=%async_computation.10 | async-start | bytes 5308416 | tf_op jit(solution)/shard_map/all_gather | solution.py:88
  8.0 93.8 %all-gather.11.cloned.1.call-start = ((), (), s32[]{:S(2)}) async-start(), calls=%async_computation.11 | async-start | bytes 1769472 | tf_op jit(solution)/shard_map/all_gather | solution.py:89
  8.7 132.2 %all-gather.15.cloned.1.call-start = ((), (), s32[]{:S(2)}) async-start(), calls=%async_computation.13 | async-start | bytes 1769472 | tf_op jit(solution)/shard_map/all_gather | solution.py:92
  11.4 47.3 %copy-start.36 = (f32[128]{0:T(128)}, f32[128]{0:T(128)S(1)}, u32[]{:S(2)}) copy-start(f32[128]{0:T(128)S(1)} %get-tuple-element.144) | copy-start | bytes 1540
  16.7 42.1 %copy-start.26 = (f32[768]{0:T(1024)}, f32[768]{0:T(1024)S(1)}, u32[]{:S(2)}) copy-start(f32[768]{0:T(1024)S(1)} %reshape.367) | copy-start | bytes 9220
  54.5 1.9 slice-start
  58.9 2.9 copy-start.19
  60.7 9.1 copy-start.33
  65.6 13.2 %all-to-all-start = ((bf16[128,3,12,64]{0,3,1,2:T(8,128)(2,1)}), bf16[128,3,12,64]{0,3,1,2:T(8,128)(2,1)S(1)}, u32[]{:S(2)}, u32[]{:S(2)}) async-start(bf16[128,3,12,64]{0,3,1,2:T(8,128)(2,1)} %copy.136), calls=%async_computation | async-start | bytes 1179648 | tf_op jit(solution)/shard_map/all_to_all | solution.py:102
  85.3 18.9 %copy-start.22 = (bf16[3,64,512]{2,1,0:T(8,128)(2,1)}, bf16[3,64,512]{2,1,0:T(8,128)(2,1)S(1)}, u32[]{:S(2)}) copy-start(bf16[3,64,512]{2,1,0:T(8,128)(2,1)S(1)} %fusion.19) | copy-start | bytes 589828
  88.4 9.4 all-to-all-start.1
  92.4 92.5 %all-gather.13.cloned.1.call-start = ((), (), s32[]{:S(2)}) async-start(), calls=%async_computation.12 | async-start | bytes 8355840 | tf_op jit(solution)/shard_map/all_gather | solution.py:161
  93.2 15.0 %copy-start.24 = (f32[768]{0:T(1024)}, f32[768]{0:T(1024)S(1)}, u32[]{:S(2)}) copy-start(f32[768]{0:T(1024)S(1)} %reshape.368) | copy-start | bytes 9220
  112.0 95.5 %all-gather.17.cloned.1.call-start = ((), (), s32[]{:S(2)}) async-start(), calls=%async_computation.14 | async-start | bytes 1769472 | tf_op jit(solution)/shard_map/all_gather | solution.py:93
  112.6 169.3 %all-gather.19.cloned.1.call-start = ((), (), s32[]{:S(2)}) async-start(), calls=%async_computation.16 | async-start | bytes 8355840 | tf_op jit(solution)/shard_map/all_gather | solution.py:199
  121.8 15.3 %copy-start.28 = (bf16[768,4]{0,1:T(4,128)(2,1)}, bf16[768,4]{0,1:T(4,128)(2,1)S(1)}, u32[]{:S(2)}) copy-start(bf16[768,4]{0,1:T(4,128)(2,1)S(1)} %all_gather.44) | copy-start | bytes 18436
  140.9 300.3 %reduce-scatter.10.cloned.1.call-start = ((), (), s32[]{:S(2)}) async-start(), calls=%async_computation.15 | async-start | bytes 16711680 | tf_op jit(solution)/shard_map/reduce_scatter | solution.py:165
  217.8 384.0 %reduce-scatter.12.cloned.1.call-start = ((), (), s32[]{:S(2)}) async-start(), calls=%async_computation.17 | async-start | bytes 16711680 | tf_op jit(solution)/shard_map/reduce_scatter | solution.py:210
  281.9 9.8 copy-start.8
  302.3 343.0 %reduce-scatter.16.cloned.1.call-start = ((), (), s32[]{:S(2)}) async-start(), calls=%async_computation.19 | async-start | bytes 884736 | tf_op jit(solution)/shard_map/reduce_scatter | solution.py:321
  450.0 7.0 copy-start.29
  450.0 7.0 copy-start.32
  607.1 8.9 copy-start.12
  607.1 8.9 copy-start.25
  616.0 13.8 %copy-start.23 = (bf16[3,64,512]{2,1,0:T(8,128)(2,1)S(1)}, bf16[3,64,512]{2,1,0:T(8,128)(2,1)}, u32[]{:S(2)}) copy-start(bf16[3,64,512]{2,1,0:T(8,128)(2,1)} %copy-done.22) | copy-start | bytes 589828
  631.0 45.4 %reduce-scatter.14.cloned.1.call-start = ((), (), s32[]{:S(2)}) async-start(), calls=%async_computation.18 | async-start | bytes 2654208 | tf_op jit(solution)/shard_map/reduce_scatter | solution.py:320
  636.4 1.9 copy-start.18
  640.2 212.1 %all-reduce.15.cloned.1.call-start = ((), (), s32[]{:S(2)}) async-start(), calls=%async_computation.23 | async-start | bytes 9437184 | tf_op jit(solution)/shard_map/psum | solution.py:343
  679.4 172.9 %copy-start.7 = (bf16[1280,4,192]{0,2,1:T(8,128)(2,1)S(1)}, bf16[1280,4,192]{0,2,1:T(8,128)(2,1)}, u32[]{:S(2)}) copy-start(bf16[1280,4,192]{0,2,1:T(8,128)(2,1)} %copy-done.6) | copy-start | bytes 5898244
  679.5 267.7 %reduce-scatter.22.cloned.1.call-start = ((), (), s32[]{:S(2)}) async-start(), calls=%async_computation.22 | async-start | bytes 589824
  681.7 314.7 %all-reduce.17.cloned.1.call-start = ((), (), s32[]{:S(2)}) async-start(), calls=%async_computation.24 | async-start | bytes 9437184 | tf_op jit(solution)/shard_map/psum | solution.py:342
  852.3 6.8 copy-start.44
  852.3 156.5 %reduce-scatter.18.cloned.1.call-start = ((), (), s32[]{:S(2)}) async-start(), calls=%async_computation.20 | async-start | bytes 3538944 | tf_op jit(solution)/shard_map/reduce_scatter | solution.py:324
  858.9 187.3 %reduce-scatter.20.cloned.1.call-start = ((), (), s32[]{:S(2)}) async-start(), calls=%async_computation.21 | async-start | bytes 3538944 | tf_op jit(solution)/shard_map/reduce_scatter | solution.py:325
  868.1 3.0 copy-start.14
  882.9 5.7 copy-start.10
  890.7 57.5 %all-to-all-start.2 = ((bf16[4,2,36864]{2,1,0:T(2,128)(2,1)}), bf16[4,2,36864]{2,1,0:T(2,128)(2,1)}, u32[]{:S(2)}, u32[]{:S(2)}) async-start(bf16[4,2,36864]{2,1,0:T(2,128)(2,1)} %reshape.384), calls=%async_computation.4 | async-start | bytes 1179648 | tf_op jit(solution)/shard_map/all_to_all | solution.py:296
  899.7 4.7 copy-start.40
  903.0 52.4 %copy-start.4 = (bf16[768,2304]{1,0:T(8,128)(2,1)S(1)}, bf16[768,2304]{1,0:T(8,128)(2,1)}, u32[]{:S(2)}) copy-start(bf16[768,2304]{1,0:T(8,128)(2,1)} %all-gather.9.cloned.1.call-done) | copy-start | bytes 10616836
  903.0 52.4 %copy-start.27 = (f32[768]{0:T(1024)S(1)}, f32[768]{0:T(1024)}, u32[]{:S(2)}) copy-start(f32[768]{0:T(1024)} %copy-done.26) | copy-start | bytes 9220
  952.1 7.1 copy-start.31
  996.4 50.8 %copy-start.1 = (f32[12,32]{1,0:T(8,128)S(1)}, f32[12,32]{1,0:T(8,128)}, u32[]{:S(2)}) copy-start(f32[12,32]{1,0:T(8,128)} %param.19) | copy-start | bytes 4612
  996.4 49.8 %copy-start.20 = (f32[768,384]{1,0:T(8,128)S(1)}, f32[768,384]{1,0:T(8,128)}, u32[]{:S(2)}) copy-start(f32[768,384]{1,0:T(8,128)} %get-tuple-element.161) | copy-start | bytes 3538948
  (16 other events, 16.0 us)
Sparse Core Ops, SparseCore 0:
  9.6 52.0 all-gather.8
  63.3 22.7 all-gather.10
  87.7 22.7 all-gather.14
  113.3 71.5 all-gather.12
  186.3 21.1 all-gather.16
  210.2 71.5 all-gather.18
  286.0 155.1 reduce-scatter.9
  445.8 155.9 reduce-scatter.11
  631.1 14.1 reduce-scatter.15
  648.1 28.2 reduce-scatter.13
  680.0 172.2 all-reduce.14
  854.4 12.0 reduce-scatter.21
  869.2 101.9 all-reduce.16
  973.9 34.8 reduce-scatter.17
  1011.4 34.7 reduce-scatter.19
